TPU v7x, 32 devices: a whole 2x2x4 slice. The times are simulated.
32 devices in a mesh: groups: 2 (over y), seq: 4 (over z), inner: 2 (over x), head: 2 (over core).
Axes of the slice: x: 2, y: 2, z: 4, core: 2. Of those that a mesh axis runs over, the one named last changes fastest.
Arguments:
- queries: bfloat16 [2048, 32, 128], P(('groups', 'seq', 'inner'), 'head'), parts along dimension 0, as said below
- keys: bfloat16 [2048, 4, 128], P(('groups', 'seq', 'inner'), 'head'), parts along dimension 0
- values: bfloat16 [2048, 4, 128], P(('groups', 'seq', 'inner'), 'head'), parts along dimension 0, may hold values from -6 to 6
- log_decay: float32 [2048, 4], P(('groups', 'seq', 'inner'), 'head'), parts along dimension 0, as said below
- gain: float32 [32, 128], P('head'), may hold values from 0.1 to 1.9
- block_list: int32 [32, 16], P(('groups', 'seq', 'inner')), parts along dimension 0, may hold values from 0 to 15, as said below
Outputs:
- attended: bfloat16 [2048, 32, 128], P(('groups', 'seq', 'inner'), 'head'), parts along dimension 0
There are 2 independent parts, one for each index of `groups`. A program takes and returns all parts, laid end to end along the dimension named above; an argument that names none is the same for every part. Nothing has to cross between parts.
Inputs may be any that keep to these rules, and one draw needn't show every extreme that they name: Keys lie within -6 to 6; queries within -144 to 144. `log_decay`: each entry is below 0. `block_list`: entry 0 of row b is b. The sequence's pieces of 128 tokens fall into segments: piece p belongs to segment p modulo 2. Every entry of row b is a block at or before b in a piece of b's segment.
All inputs are finite; a program needn't handle non-finite values.
Results may differ from a plain program's by a relative error of at most 0.0017.
Values may be sent and summed in bfloat16 or wider, within the bound.
A program may use at most 64 MiB of HBM per device.

v0:
```python
import jax
import jax.numpy as jnp
from jax import lax
from jax.sharding import PartitionSpec as P

BLK = 64
SEL = 16
HIGH = lax.Precision.HIGHEST


def prefix(shard, axis, combine, identity):
    devices, here = (lax.axis_size(axis), lax.axis_index(axis))
    everything = jax.tree.map(lambda part: lax.all_gather(part, axis), shard)
    start = jax.tree.map(
        lambda part, zero: jnp.broadcast_to(jnp.asarray(zero, part.dtype), part.shape),
        shard,
        identity,
    )

    def turn(k, before):
        reached = k < here
        new = combine(before, jax.tree.map(lambda part: part[k], everything))
        return jax.tree.map(lambda a, b: jnp.where(reached, a, b), new, before)

    return lax.fori_loop(0, devices, turn, start)


def combine(earlier, later):
    return (earlier[0] * later[0], later[0][:, None, None] * earlier[1] + later[1])


def shards(queries, keys, values, log_decay, gain, block_list):
    tokens, heads_loc, width = queries.shape
    kv_loc = keys.shape[1]
    rep = heads_loc // kv_loc
    qf = queries.astype(jnp.float32).reshape(tokens, kv_loc, rep, width)
    kf = keys.astype(jnp.float32)
    vf = values.astype(jnp.float32)
    cum = jnp.cumsum(log_decay, axis=0)
    total = cum[-1]
    causal = jnp.arange(tokens)[:, None] >= jnp.arange(tokens)[None, :]
    scores = jnp.einsum("tkrd,skd->krts", qf, kf, precision=HIGH)
    diff = cum.T[:, :, None] - cum.T[:, None, :]
    weight = jnp.where(causal[None], jnp.exp(jnp.minimum(diff, 0.0)), 0.0)
    intra = jnp.einsum("krts,skd->tkrd", scores * weight[:, None], vf, precision=HIGH)
    tail = jnp.exp(total[None, :] - cum)
    own_state = jnp.einsum("skd,ske->kde", kf * tail[:, :, None], vf, precision=HIGH)
    own_decay = jnp.exp(total)
    identity = (jnp.ones_like(own_decay), jnp.zeros_like(own_state))
    prior = prefix((own_decay, own_state), ("seq", "inner"), combine, identity)
    prior_state = prior[1]
    inter = jnp.exp(cum)[:, :, None, None] * jnp.einsum(
        "tkrd,kde->tkre", qf, prior_state, precision=HIGH
    )
    linear = (intra + inter).reshape(tokens, heads_loc, width)
    normed = (
        linear * lax.rsqrt(jnp.mean(linear * linear, axis=-1, keepdims=True) + 1e-06) * gain[None]
    )
    per_piece = tokens // BLK
    n_inner = lax.axis_size("inner")
    start_pos = (lax.axis_index("seq") * n_inner + lax.axis_index("inner")) * tokens
    seg_block = block_list // (n_inner * per_piece) * per_piece + block_list % per_piece
    seg_keys, seg_values = (
        lax.all_gather(keys, "seq", axis=0, tiled=True),
        lax.all_gather(values, "seq", axis=0, tiled=True),
    )
    key_blocks = seg_keys.reshape(-1, BLK, kv_loc, width)
    value_blocks = seg_values.reshape(-1, BLK, kv_loc, width)
    picked_keys = key_blocks[seg_block]
    picked_values = value_blocks[seg_block]
    lower = jnp.arange(SEL)[None, :] < jnp.arange(SEL)[:, None]
    repeat = jnp.any((block_list[:, :, None] == block_list[:, None, :]) & lower[None], axis=2)
    keep_all = jnp.logical_not(repeat)
    query_pos = start_pos + jnp.arange(tokens).reshape(per_piece, BLK)
    key_pos = block_list[:, :, None] * BLK + jnp.arange(BLK)[None, None, :]
    q_blocks = queries.reshape(per_piece, BLK, kv_loc, rep, width)

    def one_block(args):
        qblk, pk, pv, qpos, kpos, keep = args
        valid = keep[None, :, None] & (kpos[None] <= qpos[:, None, None])
        score = jnp.einsum(
            "qkrd,jukd->krqju", qblk, pk, preferred_element_type=jnp.float32
        ) * width ** (-0.5)
        score = jnp.where(valid[None, None], score, -1e30)
        top = jnp.max(score, axis=(3, 4), keepdims=True)
        expo = jnp.where(valid[None, None], jnp.exp(score - top), 0.0)
        denom = jnp.sum(expo, axis=(3, 4))
        weights = expo.astype(jnp.bfloat16)
        out = jnp.einsum("krqju,jukd->qkrd", weights, pv, preferred_element_type=jnp.float32)
        return out / jnp.transpose(denom, (2, 0, 1))[:, :, :, None]

    outs = lax.map(one_block, (q_blocks, picked_keys, picked_values, query_pos, key_pos, keep_all))
    sparse = outs.reshape(tokens, heads_loc, width)
    return (normed + sparse).astype(jnp.bfloat16)


def solution(mesh):
    return jax.shard_map(
        shards,
        mesh=mesh,
        in_specs=(
            P(("groups", "seq", "inner"), "head", None),
            P(("groups", "seq", "inner"), "head", None),
            P(("groups", "seq", "inner"), "head", None),
            P(("groups", "seq", "inner"), "head"),
            P("head", None),
            P(("groups", "seq", "inner"), None),
        ),
        out_specs=P(("groups", "seq", "inner"), "head", None),
        check_vma=False,
    )
```

profile of v0, /device:TPU:0, one launch (start us, length us, event | category | flops | bytes accessed | tf_op | source)
XLA Modules:
  0.0 109.6 jit_solution(16745564901405145584)
XLA Ops:
  6.5 0.8 copy.113
  8.1 1.0 convert_multiply_fusion
  9.2 1.8 %fusion.30 = f32[2,128,128]{2,1,0:T(8,128)} fusion(f32[128,2,128]{2,1,0:T(2,128)S(1)} %convert_multiply_fusion, bf16[128,2,128]{2,1,0:T(2,128)(2,1)} %param.12), kind=kOutput, calls=%fused_computation.44 | convolution fusion | flops 50331648 | bytes 327680 | tf_op jit(solution)/shard_map/skd,ske->kde/dot_general | solution.py:47
  11.0 0.9 copy.121
  11.9 0.9 copy.129
  12.7 16.1 %all_gather.19 = bf16[512,2,128]{2,0,1:T(8,128)(2,1)S(1)} all-gather(bf16[128,2,128]{2,0,1:T(8,128)(2,1)S(1)} %copy.121), channel_id=1, replica_groups=mesh['groups'=2,'seq'=4,'inner'=2,'head'=2] {'seq'}, dimensions={0}, use_global_device_ids=true | all-gather | bytes 327680 | tf_op jit(solution)/shard_map/all_gather | solution.py:65
  29.6 0.9 and_reduce_fusion
  31.8 15.7 %all_gather.20 = bf16[512,2,128]{2,0,1:T(8,128)(2,1)S(1)} all-gather(bf16[128,2,128]{2,0,1:T(8,128)(2,1)S(1)} %copy.129), channel_id=1, replica_groups=mesh['groups'=2,'seq'=4,'inner'=2,'head'=2] {'seq'}, dimensions={0}, use_global_device_ids=true | all-gather | bytes 327680 | tf_op jit(solution)/shard_map/all_gather | solution.py:64
  47.5 0.7 gather_fusion
  48.2 0.9 gather_fusion.1
  49.2 18.8 %while.24 = (s32[]{:T(128)}, f32[2,64,2,8,128]{4,3,2,1,0:T(8,128)S(1)}, bf16[2,16,64,2,128]{4,2,3,1,0:T(8,128)(2,1)S(1)}, pred[2,16]{1,0:T(4,128)(4,1)}, s32[2,1...) while((s32[]{:T(128)}, ...), condition=%wide.region_8.9_spmd, body=%wide.region_5.8_spmd.sunk | while | flops 550762496 | bytes 18383788 | solution.py:92
  50.8 1.0 constant_dynamic-slice_fusion.7
  51.8 1.8 %fusion.49 = (f32[2,8,64]{2,1,0:T(8,128)S(1)}, f32[2,16,64,64,8]{3,2,4,1,0:T(8,128)S(1)}) fusion(pred[64,16,64]{0,2,1:T(8,128)(4,1)S(1)} %compare_and_fusion.2, bf16[1,64,2,8,128]{4,3,2,1,0:T(8,128)(2,1)S(1)} %constant_dynamic-slice_fusion.7, bf16[1,16,64,2,128]{4,2,3,1,0:T(8,128)(2,1)S(1)} %get-tuple-element.348), kind=kOutput, calls=%fused_computation.4.clone.1 | convolution fusion | flops 271580160 | bytes 5050368 | tf_op jit(solution)/shard_map/while/body/eval_jaxpr/qkrd,jukd->krqju/dot_general | solution.py:81
  53.6 2.3 %fusion.50 = f32[2,8,64]{2,1,0:T(8,128)S(1)} fusion(f32[2,16,64,64,8]{3,2,4,1,0:T(8,128)S(1)} %get-tuple-element.349, f32[2,8,64]{2,1,0:T(8,128)S(1)} %get-tuple-element.350, pred[64,16,64]{0,2,1:T(8,128)(4,1)S(1)} %compare_and_fusion.2), kind=kLoop, calls=%fused_computation.5.clone.1 | loop fusion | flops 5241856 | bytes 4268032 | tf_op jit(solution)/shard_map/while/body/eval_jaxpr/reduce_sum | solution.py:87
  55.9 2.3 %fusion.51 = f32[1,64,2,8,128]{4,1,3,2,0:T(8,128)S(1)} fusion(f32[2,16,64,64,8]{3,2,4,1,0:T(8,128)S(1)} %get-tuple-element.349, f32[2,8,64]{2,1,0:T(8,128)S(1)} %get-tuple-element.350, pred[64,16,64]{0,2,1:T(8,128)(4,1)S(1)} %compare_and_fusion.2, bf16[1,16,64,2,128]{4,2,3,1,0:T(8,128)(2,1)S(1)} %get-tuple-element.351, f32[64,2,8]{0,2,1:T(8,128)S(1)} %bitcast.148), kind=kOutput, calls=%fused_computation.11.clone.1 | convolution fusion | flops 273809408 | bytes 5316608 | tf_op jit(solution)/shard_map/while/body/eval_jaxpr/krqju,jukd->qkrd/dot_general | solution.py:89
  60.2 1.0 constant_dynamic-slice_fusion.7
  61.2 1.8 %fusion.49 = (f32[2,8,64]{2,1,0:T(8,128)S(1)}, f32[2,16,64,64,8]{3,2,4,1,0:T(8,128)S(1)}) fusion(pred[64,16,64]{0,2,1:T(8,128)(4,1)S(1)} %compare_and_fusion.2, bf16[1,64,2,8,128]{4,3,2,1,0:T(8,128)(2,1)S(1)} %constant_dynamic-slice_fusion.7, bf16[1,16,64,2,128]{4,2,3,1,0:T(8,128)(2,1)S(1)} %get-tuple-element.348), kind=kOutput, calls=%fused_computation.4.clone.1 | convolution fusion | flops 271580160 | bytes 5050368 | tf_op jit(solution)/shard_map/while/body/eval_jaxpr/qkrd,jukd->krqju/dot_general | solution.py:81
  63.0 2.3 %fusion.50 = f32[2,8,64]{2,1,0:T(8,128)S(1)} fusion(f32[2,16,64,64,8]{3,2,4,1,0:T(8,128)S(1)} %get-tuple-element.349, f32[2,8,64]{2,1,0:T(8,128)S(1)} %get-tuple-element.350, pred[64,16,64]{0,2,1:T(8,128)(4,1)S(1)} %compare_and_fusion.2), kind=kLoop, calls=%fused_computation.5.clone.1 | loop fusion | flops 5241856 | bytes 4268032 | tf_op jit(solution)/shard_map/while/body/eval_jaxpr/reduce_sum | solution.py:87
  65.3 2.3 %fusion.51 = f32[1,64,2,8,128]{4,1,3,2,0:T(8,128)S(1)} fusion(f32[2,16,64,64,8]{3,2,4,1,0:T(8,128)S(1)} %get-tuple-element.349, f32[2,8,64]{2,1,0:T(8,128)S(1)} %get-tuple-element.350, pred[64,16,64]{0,2,1:T(8,128)(4,1)S(1)} %compare_and_fusion.2, bf16[1,16,64,2,128]{4,2,3,1,0:T(8,128)(2,1)S(1)} %get-tuple-element.351, f32[64,2,8]{0,2,1:T(8,128)S(1)} %bitcast.148), kind=kOutput, calls=%fused_computation.11.clone.1 | convolution fusion | flops 273809408 | bytes 5316608 | tf_op jit(solution)/shard_map/while/body/eval_jaxpr/krqju,jukd->qkrd/dot_general | solution.py:89
  68.0 20.6 %all-gather.1 = f32[8,1,2]{2,1,0:T(1,128)S(1)} all-gather(f32[1,1,2]{2,1,0:T(1,128)S(1)} %copy-done.4), channel_id=1, replica_groups=mesh['groups'=2,'seq'=4,'inner'=2,'head'=2] {'seq','inner'}, dimensions={0}, use_global_device_ids=true | all-gather | bytes 72 | tf_op jit(solution)/shard_map/all_gather | solution.py:13
  88.9 1.4 %fusion.26 = f32[2,8,128,128]{2,3,1,0:T(8,128)S(1)} fusion(f32[2,128,128]{1,2,0:T(8,128)S(1)} %exponential_select_fusion.1, bf16[128,2,8,128]{3,2,1,0:T(8,128)(2,1)} %bitcast.138, bf16[128,2,128,1]{2,1,0,3:T(2,128)(2,1)S(1)} %bitcast.144), kind=kOutput, calls=%fused_computation.38 | convolution fusion | flops 67371008 | bytes 1769472 | tf_op jit(solution)/shard_map/tkrd,skd->krts/dot_general | solution.py:42
  91.0 8.3 %while.25 = (s32[]{:T(128)}, f32[2,128,128]{2,1,0:T(8,128)S(1)}, s32[]{:T(128)}, f32[8,2]{1,0:T(8,128)S(1)}, f32[8,2,128,128]{3,2,1,0:T(8,128)}, /*index=5*/s32[]{:T(128)}, s32[]{:T(128)}) while((s32[]{:T(128)}, f32[2,128,128]{2,1,0:T(8,128)S(1)}, s32[]{:T(128)}, f32[8,2]{1,0:T(8,128)S(1)}, f32[8,2,128,128]{3,2,1,0:T(8,128)}, ...), condition=%wide.region_2.3_spmd.clone, body=%wide.region_1.2_spmd.clone.sunk | while | flops 131076 | bytes 393353 | solution.py:25
  91.0 1.0 fusion.52
  92.0 1.0 fusion.52
  93.1 1.0 fusion.52
  94.1 1.0 fusion.52
  95.1 1.0 fusion.52
  96.2 1.0 fusion.52
  97.2 1.0 fusion.52
  98.2 1.0 fusion.52
  99.2 1.8 %multiply_reduce_fusion = (f32[128,2,8]{0,2,1:T(8,128)S(1)}, f32[128,2,8,128]{0,3,2,1:T(8,128)S(1)}) fusion(f32[128,2,8,128]{0,3,2,1:T(8,128)S(1)} %convolution_bitcast_fusion.2, bf16[128,2,8,128]{3,2,1,0:T(8,128)(2,1)} %bitcast.139, f32[2,128,128]{2,1,0:T(8,128)S(1)} %get-tuple-element.141, f32[128,2]{0,1:T(2,128)S(1)} %copy.118), kind=kOutput, calls=%fused_computation.40 | convolution fusion | flops 403699712 | bytes 2761728 | tf_op jit(solution)/shard_map/tkrd,kde->tkre/dot_general | solution.py:52
  101.6 1.1 %add_convert_fusion = bf16[128,16,128]{2,1,0:T(8,128)(2,1)} fusion(f32[128,16,128]{2,1,0:T(8,128)S(1)} %bitcast.143, f32[128,16,128]{2,1,0:T(8,128)S(1)} %copy.126, f32[16,128]{1,0:T(8,128)S(1)} %copy-done.3, f32[128,16]{1,0:T(8,128)S(1)} %copy.125), kind=kLoop, calls=%fused_computation.39 | loop fusion | flops 1048576 | bytes 2637824 | tf_op jit(solution)/shard_map/convert_element_type | solution.py:94
  (55 shorter events, 8.6 us)
Async XLA Ops:
  6.5 84.4 %all-gather.4.cloned.1.call-start = ((), (), s32[]{:S(2)}) async-start(), calls=%async_computation | async-start | bytes 1179648 | tf_op jit(solution)/shard_map/all_gather | solution.py:13
  29.6 17.9 %copy-start.2 = (s32[1024]{0:T(1024)}, s32[1024]{0:T(1024)S(1)}, u32[]{:S(2)}) copy-start(s32[1024]{0:T(1024)S(1)} %pad_clamp_fusion) | copy-start | bytes 12292
  49.1 18.8 %copy-start.4 = (f32[1,1,2]{2,1,0:T(1,128)S(1)}, f32[1,1,2]{2,1,0:T(1,128)}, u32[]{:S(2)}) copy-start(f32[1,1,2]{2,1,0:T(1,128)} %get-tuple-element.264) | copy-start | bytes 28
  49.1 39.7 %copy-start = (bf16[128,2,128]{2,1,0:T(2,128)(2,1)S(1)}, bf16[128,2,128]{2,1,0:T(2,128)(2,1)}, u32[]{:S(2)}) copy-start(bf16[128,2,128]{2,1,0:T(2,128)(2,1)} %param.11) | copy-start | bytes 196612
  49.2 41.1 %copy-start.1 = (bf16[128,2,128]{2,1,0:T(2,128)(2,1)S(1)}, bf16[128,2,128]{2,1,0:T(2,128)(2,1)}, u32[]{:S(2)}) copy-start(bf16[128,2,128]{2,1,0:T(2,128)(2,1)} %param.12) | copy-start | bytes 196612
  67.9 33.7 %copy-start.3 = (f32[16,128]{1,0:T(8,128)S(1)}, f32[16,128]{1,0:T(8,128)}, u32[]{:S(2)}) copy-start(f32[16,128]{1,0:T(8,128)} %param.14) | copy-start | bytes 24580
Sparse Core Ops, SparseCore 0:
  11.1 43.3 all-gather.3
where the time goes:
time: 110 us
  blocking collectives  52.4 us (48%)
  other arithmetic  18.3 us (17%)
  matrix products  13.7 us (12%)
  between operations  13.6 us (12%)
  local copies, waits for them, and re-layouts  11.2 us (10%)
    all_gather x1, blocking collectives, prefix(): everything = jax.tree.map(lambda part: lax.all_gather(part, axis), shard)  20.6 us
    all_gather x1, blocking collectives, shards(): lax.all_gather(values, 'seq', axis=0, tiled=True)  16.1 us
    all_gather x1, blocking collectives, shards(): lax.all_gather(keys, 'seq', axis=0, tiled=True)  15.7 us
    select_n x8, other arithmetic, turn(): return jax.tree.map(lambda a, b: jnp.where(reached, a, b), new, before)  7.94 us
    dot_general x2, matrix products, one_block(): jnp.einsum('krqju,jukd->qkrd', weights, pv, preferred_element_type=jnp.fl...  4.6 us
    reduce_sum x2, other arithmetic, one_block(): denom = jnp.sum(expo, axis=(3, 4))  4.54 us
    dot_general x2, matrix products, one_block(): jnp.einsum('qkrd,jukd->krqju', qblk, pk, preferred_element_type=jnp.float32)  3.54 us
    unnamed x13, local copies, waits for them, and re-layouts  2.52 us
  transfers between devices with their start and end apart: 1, of which 0 were waited for; matrix products, arithmetic and copies ran while one was open for 25% of the time, Pallas kernels for 0%

commit v1 on v0

--- a/solution.py
+++ b/solution.py
@@ -6,6 +6,28 @@
 BLK = 64
 SEL = 16
 HIGH = lax.Precision.HIGHEST
+
+
+def joined_along(blocks, dim):
+    blocks = jnp.moveaxis(blocks, 0, dim)
+    lengths = blocks.shape
+    return blocks.reshape(*lengths[:dim], lengths[dim] * lengths[dim + 1], *lengths[dim + 2 :])
+
+
+def ring_gather(x, axis, dim):
+    size = lax.axis_size(axis)
+    pairs = [(i, (i + 1) % size) for i in range(size)]
+    back = [(b, a) for a, b in pairs]
+    lower, upper = ([], [])
+    for turn in range(size - 1):
+        if turn % 2 == 0:
+            lower.append(lax.ppermute(lower[-1] if lower else x, axis, pairs))
+        else:
+            upper.append(lax.ppermute(upper[-1] if upper else x, axis, back))
+    parts = jnp.stack([*lower[::-1], x, *upper])
+    shift = lax.axis_index(axis) - len(lower)
+    parts = parts[(jnp.arange(size) - shift) % size]
+    return joined_along(parts, dim)
 
 
 def prefix(shard, axis, combine, identity):
@@ -62,7 +84,7 @@
     seg_block = block_list // (n_inner * per_piece) * per_piece + block_list % per_piece
     seg_keys, seg_values = (
         lax.all_gather(keys, "seq", axis=0, tiled=True),
-        lax.all_gather(values, "seq", axis=0, tiled=True),
+        ring_gather(values, "seq", 0),
     )
     key_blocks = seg_keys.reshape(-1, BLK, kv_loc, width)
     value_blocks = seg_values.reshape(-1, BLK, kv_loc, width)

time: 110 us -> 105 us (0.955)
  blocking collectives: 52.4 us -> 36.1 us
  waiting for transfers between devices: 0.04 us -> 6.05 us
  starting transfers between devices: 0.01 us -> 5.19 us
  local copies, waits for them, and re-layouts: 11.2 us -> 8.55 us
  matrix products: 13.7 us -> 15.8 us
    all_gather x1 -> x0, blocking collectives: 16.1 us -> none  [shards(): lax.all_gather(values, 'seq', axis=0, tiled=True)]
    ppermute x0 -> x3, waiting for transfers between devices: none -> 6.03 us  [the longest x2 6.03 us: ring_gather(): lower.append(lax.ppermute(lower[-1] if lower else x, axis, pairs))]
    ppermute x0 -> x3, starting transfers between devices: none -> 5.19 us  [the longest x1 5.13 us: ring_gather(): upper.append(lax.ppermute(upper[-1] if upper else x, axis, back))]
    while x0 -> x8, local copies, waits for them, and re-layouts: none -> 1.99 us
    dynamic_slice x4, local copies, waits for them, and re-layouts: 2.11 us -> 0.21 us  [shards(): lax.map(one_block, (q_blocks, picked_keys, picked_values, query_pos, key_...]
    dot_general x1, matrix products: 0.68 us -> 2.54 us  [shards(): jnp.einsum('krts,skd->tkrd', scores * weight[:, None], vf, precision=HIGH)]
    le x4, local copies, waits for them, and re-layouts: 1.38 us -> 0.02 us  [one_block(): valid = keep[None, :, None] & (kpos[None] <= qpos[:, None, None])]
    and x2, local copies, waits for them, and re-layouts: 1.34 us -> 0.02 us  [one_block(): valid = keep[None, :, None] & (kpos[None] <= qpos[:, None, None])]
  transfers between devices with their start and end apart: 1 -> 4, of which waited for: 0 -> 1; matrix products, arithmetic and copies ran while one was open for 25% -> 26% of each run, Pallas kernels for 0% -> 0%
where the time goes in v1:
time: 105 us; the launch traced here: 104 us
  blocking collectives  36.1 us (34%)
  other arithmetic  18.4 us (18%)
  matrix products  15.8 us (15%)
  between operations  13.6 us (13%)
  local copies, waits for them, and re-layouts  8.55 us (8%)
  waiting for transfers between devices  6.05 us (6%)
  starting transfers between devices  5.19 us (5%)
    all_gather x1, blocking collectives, prefix(): everything = jax.tree.map(lambda part: lax.all_gather(part, axis), shard)  21.2 us
    all_gather x1, blocking collectives, shards(): lax.all_gather(keys, 'seq', axis=0, tiled=True)  15 us
    select_n x8, other arithmetic, turn(): return jax.tree.map(lambda a, b: jnp.where(reached, a, b), new, before)  7.94 us
    ppermute x2, waiting for transfers between devices, ring_gather(): lower.append(lax.ppermute(lower[-1] if lower else x, axis, pairs))  6.03 us
    ppermute x1, starting transfers between devices, ring_gather(): upper.append(lax.ppermute(upper[-1] if upper else x, axis, back))  5.13 us
    dot_general x2, matrix products, one_block(): jnp.einsum('krqju,jukd->qkrd', weights, pv, preferred_element_type=jnp.fl...  4.55 us
    reduce_sum x2, other arithmetic, one_block(): denom = jnp.sum(expo, axis=(3, 4))  4.53 us
    dot_general x2, matrix products, one_block(): jnp.einsum('qkrd,jukd->krqju', qblk, pk, preferred_element_type=jnp.float32)  3.55 us
  transfers between devices with their start and end apart: 4, of which 1 were waited for; matrix products, arithmetic and copies ran while one was open for 26% of the time, Pallas kernels for 0%

profile of v1, /device:TPU:0, one launch (start us, length us, event | category | flops | bytes accessed | tf_op | source)
XLA Modules:
  0.0 104.1 jit_solution(13668913398350411721)
XLA Ops:
  6.5 0.9 copy.221
  7.4 5.1 %collective-permute-start.2 = (bf16[128,2,128]{2,0,1:T(8,128)(2,1)S(1)}, bf16[128,2,128]{2,0,1:T(8,128)(2,1)S(1)}, u32[]{:S(2)}, u32[]{:S(2)}) collective-permute-start(bf16[128,2,128]{2,0,1:T(8,128)(2,1)S(1)} %copy.221), channel_id=1, source_target_pairs={{4,0},{8,4},{12,8},{0,12},{5,1},{9,5},{13,9},{1,13},{6,2},{10,6},{... | collective-permute-start | bytes 196616 | tf_op jit(solution)/shard_map/ppermute | solution.py:26
  12.6 0.8 copy.143
  13.6 1.0 convert_multiply_fusion
  14.6 1.8 %fusion.30 = f32[2,128,128]{2,1,0:T(8,128)} fusion(f32[128,2,128]{2,1,0:T(2,128)S(1)} %convert_multiply_fusion, bf16[128,2,128]{2,1,0:T(2,128)(2,1)} %param.12), kind=kOutput, calls=%fused_computation.46 | convolution fusion | flops 50331648 | bytes 327680 | tf_op jit(solution)/shard_map/skd,ske->kde/dot_general | solution.py:69
  16.5 0.9 copy.162
  18.2 0.9 and_reduce_fusion
  19.2 15.0 %all_gather.16 = bf16[512,2,128]{2,0,1:T(8,128)(2,1)S(1)} all-gather(bf16[128,2,128]{2,0,1:T(8,128)(2,1)S(1)} %copy.162), channel_id=1, replica_groups=mesh['groups'=2,'seq'=4,'inner'=2,'head'=2] {'seq'}, dimensions={0}, use_global_device_ids=true | all-gather | bytes 327680 | tf_op jit(solution)/shard_map/all_gather | solution.py:86
  34.2 21.2 %all-gather.1 = f32[8,1,2]{2,1,0:T(1,128)S(1)} all-gather(f32[1,1,2]{2,1,0:T(1,128)S(1)} %get-tuple-element.277), channel_id=1, replica_groups=mesh['groups'=2,'seq'=4,'inner'=2,'head'=2] {'seq','inner'}, dimensions={0}, use_global_device_ids=true | all-gather | bytes 72 | tf_op jit(solution)/shard_map/all_gather | solution.py:35
  56.4 1.4 %fusion.26 = f32[2,8,128,128]{2,3,1,0:T(8,128)S(1)} fusion(f32[2,128,128]{1,2,0:T(8,128)S(1)} %exponential_select_fusion.1, bf16[128,2,8,128]{3,2,1,0:T(8,128)(2,1)} %bitcast.145, bf16[128,2,128,1]{2,1,0,3:T(2,128)(2,1)} %bitcast.152), kind=kOutput, calls=%fused_computation.39 | convolution fusion | flops 67371008 | bytes 1769472 | tf_op jit(solution)/shard_map/tkrd,skd->krts/dot_general | solution.py:64
  57.8 2.5 %convolution_bitcast_fusion.2 = f32[128,2,8,128]{0,3,2,1:T(8,128)} fusion(f32[2,8,128,128]{2,3,1,0:T(8,128)S(1)} %fusion.26, bf16[128,2,128,1]{2,1,0,3:T(2,128)(2,1)} %bitcast.153), kind=kOutput, calls=%fused_computation.38 | convolution fusion | flops 402653184 | bytes 2162688 | tf_op jit(solution)/shard_map/krts,skd->tkrd/dot_general | solution.py:67
  60.4 6.0 %collective-permute-done.1 = bf16[128,2,128]{2,0,1:T(8,128)(2,1)S(1)} collective-permute-done((bf16[128,2,128]{2,0,1:T(8,128)(2,1)S(1)}, bf16[128,2,128]{2,0,1:T(8,128)(2,1)S(1)}, u32[]{:S(2)}, u32[]{:S(2)}) %collective-permute-start.1) | collective-permute-done | bytes 65568 | tf_op jit(solution)/shard_map/ppermute | solution.py:24
  67.9 16.2 %while.24 = (s32[]{:T(128)}, f32[2,64,2,8,128]{4,3,2,1,0:T(8,128)}, bf16[2,16,64,2,128]{4,2,3,1,0:T(8,128)(2,1)S(1)}, pred[2,16]{1,0:T(4,128)(4,1)S(1)}, s32[2,1...) while((s32[]{:T(128)}, f32[2,64,2,8,128]{4,3,2,1,0:T(8,128)}, ...), condition=%wide.region_8.9_spmd, body=%wide.region_5.8_spmd.sunk | while | flops 550762496 | bytes 26772452 | solution.py:114
  68.3 1.8 %fusion.51 = (f32[2,8,64]{2,1,0:T(8,128)S(1)}, f32[2,16,64,64,8]{3,2,4,1,0:T(8,128)S(1)}) fusion(pred[64,16,64]{0,2,1:T(8,128)(4,1)S(1)} %compare_and_fusion.2, bf16[1,64,2,8,128]{4,3,2,1,0:T(8,128)(2,1)S(1)} %constant_dynamic-slice_fusion.7, bf16[1,16,64,2,128]{4,2,3,1,0:T(8,128)(2,1)S(1)} %get-tuple-element.363), kind=kOutput, calls=%fused_computation.5.clone.1 | convolution fusion | flops 271580160 | bytes 5050368 | tf_op jit(solution)/shard_map/while/body/eval_jaxpr/qkrd,jukd->krqju/dot_general | solution.py:103
  70.1 2.3 %fusion.52 = f32[2,8,64]{2,1,0:T(8,128)S(1)} fusion(f32[2,16,64,64,8]{3,2,4,1,0:T(8,128)S(1)} %get-tuple-element.364, f32[2,8,64]{2,1,0:T(8,128)S(1)} %get-tuple-element.365, pred[64,16,64]{0,2,1:T(8,128)(4,1)S(1)} %compare_and_fusion.2), kind=kLoop, calls=%fused_computation.6.clone.1 | loop fusion | flops 5241856 | bytes 4268032 | tf_op jit(solution)/shard_map/while/body/eval_jaxpr/reduce_sum | solution.py:109
  72.4 2.3 %fusion.53 = f32[1,64,2,8,128]{4,1,3,2,0:T(8,128)S(1)} fusion(f32[2,16,64,64,8]{3,2,4,1,0:T(8,128)S(1)} %get-tuple-element.364, f32[2,8,64]{2,1,0:T(8,128)S(1)} %get-tuple-element.365, pred[64,16,64]{0,2,1:T(8,128)(4,1)S(1)} %compare_and_fusion.2, bf16[1,16,64,2,128]{4,2,3,1,0:T(8,128)(2,1)S(1)} %get-tuple-element.366, f32[64,2,8]{0,2,1:T(8,128)S(1)} %bitcast.157), kind=kOutput, calls=%fused_computation.12.clone.1 | convolution fusion | flops 273809408 | bytes 5316608 | tf_op jit(solution)/shard_map/while/body/eval_jaxpr/krqju,jukd->qkrd/dot_general | solution.py:111
  75.0 1.0 copy-done.2
  76.4 1.8 %fusion.51 = (f32[2,8,64]{2,1,0:T(8,128)S(1)}, f32[2,16,64,64,8]{3,2,4,1,0:T(8,128)S(1)}) fusion(pred[64,16,64]{0,2,1:T(8,128)(4,1)S(1)} %compare_and_fusion.2, bf16[1,64,2,8,128]{4,3,2,1,0:T(8,128)(2,1)S(1)} %constant_dynamic-slice_fusion.7, bf16[1,16,64,2,128]{4,2,3,1,0:T(8,128)(2,1)S(1)} %get-tuple-element.363), kind=kOutput, calls=%fused_computation.5.clone.1 | convolution fusion | flops 271580160 | bytes 5050368 | tf_op jit(solution)/shard_map/while/body/eval_jaxpr/qkrd,jukd->krqju/dot_general | solution.py:103
  78.2 2.3 %fusion.52 = f32[2,8,64]{2,1,0:T(8,128)S(1)} fusion(f32[2,16,64,64,8]{3,2,4,1,0:T(8,128)S(1)} %get-tuple-element.364, f32[2,8,64]{2,1,0:T(8,128)S(1)} %get-tuple-element.365, pred[64,16,64]{0,2,1:T(8,128)(4,1)S(1)} %compare_and_fusion.2), kind=kLoop, calls=%fused_computation.6.clone.1 | loop fusion | flops 5241856 | bytes 4268032 | tf_op jit(solution)/shard_map/while/body/eval_jaxpr/reduce_sum | solution.py:109
  80.4 2.3 %fusion.53 = f32[1,64,2,8,128]{4,1,3,2,0:T(8,128)S(1)} fusion(f32[2,16,64,64,8]{3,2,4,1,0:T(8,128)S(1)} %get-tuple-element.364, f32[2,8,64]{2,1,0:T(8,128)S(1)} %get-tuple-element.365, pred[64,16,64]{0,2,1:T(8,128)(4,1)S(1)} %compare_and_fusion.2, bf16[1,16,64,2,128]{4,2,3,1,0:T(8,128)(2,1)S(1)} %get-tuple-element.366, f32[64,2,8]{0,2,1:T(8,128)S(1)} %bitcast.157), kind=kOutput, calls=%fused_computation.12.clone.1 | convolution fusion | flops 273809408 | bytes 5316608 | tf_op jit(solution)/shard_map/while/body/eval_jaxpr/krqju,jukd->qkrd/dot_general | solution.py:111
  83.1 1.0 copy-done.2
  84.1 8.3 %while.25 = (s32[]{:T(128)}, f32[2,128,128]{2,1,0:T(8,128)S(1)}, s32[]{:T(128)}, f32[8,2]{1,0:T(8,128)S(1)}, f32[8,2,128,128]{3,2,1,0:T(8,128)}, /*index=5*/s32[]{:T(128)}, s32[]{:T(128)}) while((s32[]{:T(128)}, f32[2,128,128]{2,1,0:T(8,128)S(1)}, s32[]{:T(128)}, f32[8,2]{1,0:T(8,128)S(1)}, f32[8,2,128,128]{3,2,1,0:T(8,128)}, ...), condition=%wide.region_2.3_spmd.clone, body=%wide.region_1.2_spmd.clone.sunk | while | flops 131076 | bytes 393353 | solution.py:47
  84.1 1.0 fusion.54
  85.1 1.0 fusion.54
  86.2 1.0 fusion.54
  87.2 1.0 fusion.54
  88.2 1.0 fusion.54
  89.3 1.0 fusion.54
  90.3 1.0 fusion.54
  91.4 1.0 fusion.54
  92.4 1.9 %multiply_reduce_fusion = (f32[128,2,8]{0,2,1:T(8,128)S(1)}, f32[128,2,8,128]{0,3,2,1:T(8,128)S(1)}) fusion(f32[128,2,8,128]{0,3,2,1:T(8,128)} %convolution_bitcast_fusion.2, bf16[128,2,8,128]{3,2,1,0:T(8,128)(2,1)S(1)} %bitcast.147, f32[2,128,128]{2,1,0:T(8,128)S(1)} %get-tuple-element.141, f32[128,2]{0,1:T(2,128)S(1)} %copy.148), kind=kOutput, calls=%fused_computation.41 | convolution fusion | flops 403699712 | bytes 2761728 | tf_op jit(solution)/shard_map/tkrd,kde->tkre/dot_general | solution.py:74
  94.9 2.4 %add_convert_fusion = bf16[128,16,128]{2,1,0:T(8,128)(2,1)} fusion(f32[128,16,128]{2,1,0:T(8,128)} %bitcast.151, f32[128,16,128]{2,1,0:T(8,128)S(1)} %copy.156, f32[16,128]{1,0:T(8,128)S(1)} %copy-done.3, f32[128,16]{1,0:T(8,128)S(1)} %copy.155), kind=kLoop, calls=%fused_computation.40 | loop fusion | flops 1048576 | bytes 2637824 | tf_op jit(solution)/shard_map/convert_element_type | solution.py:116
  (67 shorter events, 5.7 us)
Async XLA Ops:
  6.5 61.3 %copy-start = (bf16[128,16,128]{2,1,0:T(8,128)(2,1)S(1)}, bf16[128,16,128]{2,1,0:T(8,128)(2,1)}, u32[]{:S(2)}) copy-start(bf16[128,16,128]{2,1,0:T(8,128)(2,1)} %param.10) | copy-start | bytes 1572868
  6.5 77.6 %all-gather.4.cloned.1.call-start = ((), (), s32[]{:S(2)}) async-start(), calls=%async_computation | async-start | bytes 1179648 | tf_op jit(solution)/shard_map/all_gather | solution.py:35
  7.4 52.9 %collective-permute-start.2 = (bf16[128,2,128]{2,0,1:T(8,128)(2,1)S(1)}, bf16[128,2,128]{2,0,1:T(8,128)(2,1)S(1)}, u32[]{:S(2)}, u32[]{:S(2)}) collective-permute-start(bf16[128,2,128]{2,0,1:T(8,128)(2,1)S(1)} %copy.221), channel_id=1, source_target_pairs={{4,0},{8,4},{12,8},{0,12},{5,1},{9,5},{13,9},{1,13},{6,2},{10,6},{... | collective-permute-start | bytes 196616 | tf_op jit(solution)/shard_map/ppermute | solution.py:26
  12.6 47.7 %collective-permute-start = (bf16[128,2,128]{2,0,1:T(8,128)(2,1)S(1)}, bf16[128,2,128]{2,0,1:T(8,128)(2,1)S(1)}, u32[]{:S(2)}, u32[]{:S(2)}) collective-permute-start(bf16[128,2,128]{2,0,1:T(8,128)(2,1)S(1)} %copy.221), channel_id=1, source_target_pairs={{0,4},{4,8},{8,12},{12,0},{1,5},{5,9},{9,13},{13,1},{2,6},{6,10},{... | collective-permute-start | bytes 196616 | tf_op jit(solution)/shard_map/ppermute | solution.py:24
  60.3 6.1 %collective-permute-start.1 = (bf16[128,2,128]{2,0,1:T(8,128)(2,1)S(1)}, bf16[128,2,128]{2,0,1:T(8,128)(2,1)S(1)}, u32[]{:S(2)}, u32[]{:S(2)}) collective-permute-start(bf16[128,2,128]{2,0,1:T(8,128)(2,1)S(1)} %collective-permute-done), channel_id=1, source_target_pairs={{0,4},{4,8},{8,12},{12,0},{1,5},{5,9},{9,13},{13,1},{2,6},{6,10},{... | collective-permute-start | bytes 196616 | tf_op jit(solution)/shard_map/ppermute | solution.py:24
  67.9 27.1 %copy-start.3 = (f32[16,128]{1,0:T(8,128)S(1)}, f32[16,128]{1,0:T(8,128)}, u32[]{:S(2)}) copy-start(f32[16,128]{1,0:T(8,128)} %param.14) | copy-start | bytes 24580
  72.4 2.3 %copy-start.1 = (f32[2,64,2,8,128]{4,3,2,1,0:T(8,128)S(1)}, f32[2,64,2,8,128]{4,3,2,1,0:T(8,128)}, u32[]{:S(2)}) copy-start(f32[2,64,2,8,128]{4,3,2,1,0:T(8,128)} %get-tuple-element.382) | copy-start | bytes 3145732 | tf_op jit(solution)/shard_map/while
  75.0 1.0 copy-start.2
  80.4 2.3 %copy-start.1 = (f32[2,64,2,8,128]{4,3,2,1,0:T(8,128)S(1)}, f32[2,64,2,8,128]{4,3,2,1,0:T(8,128)}, u32[]{:S(2)}) copy-start(f32[2,64,2,8,128]{4,3,2,1,0:T(8,128)} %get-tuple-element.382) | copy-start | bytes 3145732 | tf_op jit(solution)/shard_map/while
  83.1 1.0 copy-start.2
Sparse Core Ops, SparseCore 0:
  16.6 42.4 all-gather.3
